TPU v7x, 32 devices: a whole 2x2x4 slice. The times are simulated.
32 devices in a mesh: dp: 16 (over z, y, x), tensor: 2 (over core).
Axes of the slice: x: 2, y: 2, z: 4, core: 2. Of those that a mesh axis runs over, the one named last changes fastest.
Arguments:
- layer_input: bfloat16 [640, 5120], P('dp', 'tensor'), may hold values from -6 to 6
- up_weight: bfloat16 [5120, 13824], P('dp', 'tensor'), may hold values from -0.078125 to 0.078125
- grad_output: bfloat16 [640, 13824], P('dp', 'tensor'), may hold values from -60 to 60
- factor_input: float32 [5120, 5120], P('dp', 'tensor'), may hold values from -4 to 15, as said below
- factor_grad: float32 [13824, 13824], P('dp', 'tensor'), may hold values from -4 to 15, as said below
- decay: float32 [1], replicated, may hold values from 0.5 to 0.95
Outputs:
- grad_weight: float32 [5120, 13824], P('dp', 'tensor')
- grad_input: bfloat16 [640, 5120], P('tensor', 'dp')
- new_factor_input: float32 [5120, 5120], P('dp', 'tensor')
- new_factor_grad: float32 [13824, 13824], P('dp', 'tensor')
Inputs may be any that keep to these rules, and one draw needn't show every extreme that they name: `factor_input`: symmetric. `factor_grad`: symmetric.
All inputs are finite; a program needn't handle non-finite values.
Results may differ from a plain program's by a relative error of at most 0.001.
Values may be sent and summed in bfloat16 or wider, within the bound.
A program may use at most 128 MiB of HBM per device.

v0:
```python
import jax
import jax.numpy as jnp
from jax import lax
from jax.sharding import PartitionSpec as P


def from_root(value, axis, source):
    kept = jnp.where(lax.axis_index(axis) == source, value, 0).astype(value.dtype)
    return lax.psum(kept, axis)


def contract_rows(left, right):
    return lax.dot_general(
        left, right, (((0,), (0,)), ((), ())), preferred_element_type=jnp.float32
    )


def contract_cols(left, right):
    return lax.dot_general(
        left, right, (((1,), (1,)), ((), ())), preferred_element_type=jnp.float32
    )


def local(layer_input, up_weight, grad_output, factor_input, factor_grad, decay):
    ratio = lax.axis_size("dp") // lax.axis_size("tensor")
    own = lax.axis_index("dp")
    owner = own // ratio
    token_total = layer_input.shape[0] * lax.axis_size("dp")
    keep = decay[0]
    blend = (1.0 - keep) / token_total
    feat_rows = up_weight.shape[0]
    unit_rows = factor_grad.shape[0]
    input_all = lax.all_gather(layer_input, "dp", axis=0, tiled=True)
    input_slice = lax.dynamic_slice_in_dim(input_all, own % ratio * feat_rows, feat_rows, 1)
    input_part = from_root(input_slice, "tensor", owner)
    gram_input = contract_rows(input_part, input_all)
    new_factor_input = keep * factor_input + blend * gram_input
    grad_all = lax.all_gather(grad_output, "dp", axis=0, tiled=True)
    grad_slice = lax.dynamic_slice_in_dim(grad_all, own % ratio * unit_rows, unit_rows, 1)
    grad_part = from_root(grad_slice, "tensor", owner)
    grad_weight = contract_rows(input_part, grad_all)
    gram_grad = contract_rows(grad_part, grad_all)
    partial_in = contract_cols(grad_all, up_weight)
    new_factor_grad = keep * factor_grad + blend * gram_grad
    grad_input = lax.psum_scatter(partial_in, "tensor", scatter_dimension=0, tiled=True).astype(
        jnp.bfloat16
    )
    return (grad_weight, grad_input, new_factor_input, new_factor_grad)


def solution(mesh):
    return jax.shard_map(
        local,
        mesh=mesh,
        in_specs=(
            P("dp", "tensor"),
            P("dp", "tensor"),
            P("dp", "tensor"),
            P("dp", "tensor"),
            P("dp", "tensor"),
            P(),
        ),
        out_specs=(P("dp", "tensor"), P("tensor", "dp"), P("dp", "tensor"), P("dp", "tensor")),
        check_vma=False,
    )
```

profile of v0, /device:TPU:0, one launch (start us, length us, event | category | flops | bytes accessed | tf_op | source)
XLA Modules:
  0.0 267.4 jit_solution(3826725555416523902)
XLA Ops:
  7.2 0.0 all-gather.3.cloned.1.call-start
  7.2 0.7 all-gather.3.cloned.1.call-update
  7.9 0.0 all-gather.5.cloned.1.call-start
  7.9 0.7 all-gather.5.cloned.1.call-update
  8.6 0.0 all-reduce.3.cloned.1.call-start
  8.7 73.8 %all-gather.3.cloned.1.call-done = bf16[640,2560]{1,0:T(8,128)(2,1)} async-done(((bf16[40,2560]{1,0:T(8,128)(2,1)}), bf16[640,2560]{1,0:T(8,128)(2,1)}) %all-gather.3.cloned.1.call-update) | async-done | bytes 3276816 | tf_op jit(solution)/shard_map/all_gather | solution.py:33
  82.5 2.1 dynamic-slice_select_fusion.1
  84.6 115.7 %all-gather.5.cloned.1.call-done = bf16[640,6912]{1,0:T(8,128)(2,1)} async-done(((bf16[40,6912]{1,0:T(8,128)(2,1)}), bf16[640,6912]{1,0:T(8,128)(2,1)}) %all-gather.5.cloned.1.call-update) | async-done | bytes 8847376 | tf_op jit(solution)/shard_map/all_gather | solution.py:38
  200.3 2.9 %dynamic-slice_select_fusion = bf16[640,864]{1,0:T(8,128)(2,1)} fusion(bf16[640,6912]{1,0:T(8,128)(2,1)} %all-gather.5.cloned.1.call-done, s32[]{:T(128)S(6)} %select_n.41, pred[]{:T(512)S(6)} %eq.7), kind=kLoop, calls=%fused_computation.3 | loop fusion | flops 552960 | bytes 2211845 | tf_op jit(solution)/shard_map/jit(_where)/select_n | solution.py:8
  203.2 0.0 all-reduce.3.cloned.1.call-update
  203.2 0.0 reduce-scatter.2.cloned.1.call-start
  203.9 11.0 %fusion.2 = f32[640,320]{1,0:T(8,128)} fusion(bf16[640,6912]{1,0:T(8,128)(2,1)} %all-gather.5.cloned.1.call-done, bf16[320,6912]{1,0:T(8,128)(2,1)} %param.7), kind=kOutput, calls=%fused_computation.6 | convolution fusion | flops 2831155200 | bytes 14090240 | tf_op jit(solution)/shard_map/dot_general | solution.py:19
  214.9 0.0 reduce-scatter.2.cloned.1.call-update
  214.9 7.2 %all-reduce.3.cloned.1.call-done = (bf16[640,320]{1,0:T(8,128)(2,1)}, bf16[640,864]{1,0:T(8,128)(2,1)}) async-done(((bf16[640,320]{1,0:T(8,128)(2,1)}, bf16[640,864]{1,0:T(8,128)(2,1)}), (bf16[640,320]{1,0:T(8,128)(2,1)}, bf16[640,864]{1,0:T(8,128)(2,1)})) %all-reduce.3.cloned.1.call-update) | async-done | bytes 1515536 | tf_op jit(solution)/shard_map/psum | solution.py:9
  222.1 0.0 copy-start
  222.1 21.0 %multiply_add_fusion = f32[864,6912]{1,0:T(8,128)} fusion(f32[864,6912]{1,0:T(8,128)} %param.10, bf16[640,864]{1,0:T(8,128)(2,1)} %get-tuple-element.5, bf16[640,6912]{1,0:T(8,128)(2,1)} %all-gather.5.cloned.1.call-done, f32[]{:T(128)S(6)} %div.14, f32[]{:T(128)} %bitcast.11), kind=kOutput, calls=%fused_computation | convolution fusion | flops 7662034944 | bytes 57729032 | tf_op jit(solution)/shard_map/dot_general | solution.py:13
  243.1 0.0 copy-done
  243.1 0.0 copy-start.1
  243.1 5.3 %fusion = f32[320,2560]{1,0:T(8,128)} fusion(bf16[640,320]{1,0:T(8,128)(2,1)} %get-tuple-element.4, bf16[640,2560]{1,0:T(8,128)(2,1)} %all-gather.3.cloned.1.call-done, f32[320,2560]{1,0:T(8,128)S(1)} %copy-done, f32[]{:T(128)S(6)} %div.14, f32[]{:T(128)} %bitcast.9), kind=kOutput, calls=%fused_computation.2 | convolution fusion | flops 1051033600 | bytes 10240008 | tf_op jit(solution)/shard_map/dot_general | solution.py:13
  248.4 0.0 copy-done.1
  248.4 10.7 %fusion.1 = f32[320,6912]{1,0:T(8,128)} fusion(bf16[640,320]{1,0:T(8,128)(2,1)S(1)} %copy-done.1, bf16[640,6912]{1,0:T(8,128)(2,1)} %all-gather.5.cloned.1.call-done), kind=kOutput, calls=%fused_computation.5 | convolution fusion | flops 2831155200 | bytes 18104320 | tf_op jit(solution)/shard_map/dot_general | solution.py:13
  259.1 0.0 reduce-scatter.2.cloned.1.call-done
  259.1 1.8 convert_element_type.7
Async XLA Ops:
  7.2 75.3 %all-gather.3.cloned.1.call-start = ((), (), s32[]{:S(2)}) async-start(), calls=%async_computation.1 | async-start | bytes 3481600 | tf_op jit(solution)/shard_map/all_gather | solution.py:33
  7.9 192.4 %all-gather.5.cloned.1.call-start = ((), (), s32[]{:S(2)}) async-start(), calls=%async_computation.2 | async-start | bytes 9400320 | tf_op jit(solution)/shard_map/all_gather | solution.py:38
  8.6 213.4 %all-reduce.3.cloned.1.call-start = ((), (), s32[]{:S(2)}) async-start(), calls=%async_computation.4 | async-start | bytes 3276800 | tf_op jit(solution)/shard_map/psum | solution.py:9
  203.2 55.9 %reduce-scatter.2.cloned.1.call-start = ((), (), s32[]{:S(2)}) async-start(), calls=%async_computation.3 | async-start | bytes 1474560 | tf_op jit(solution)/shard_map/reduce_scatter | solution.py:45
  222.1 21.0 %copy-start = (f32[320,2560]{1,0:T(8,128)S(1)}, f32[320,2560]{1,0:T(8,128)}, u32[]{:S(2)}) copy-start(f32[320,2560]{1,0:T(8,128)} %param.9) | copy-start | bytes 9830404
  243.1 5.3 %copy-start.1 = (bf16[640,320]{1,0:T(8,128)(2,1)S(1)}, bf16[640,320]{1,0:T(8,128)(2,1)}, u32[]{:S(2)}) copy-start(bf16[640,320]{1,0:T(8,128)(2,1)} %get-tuple-element.4) | copy-start | bytes 1228804
Sparse Core Ops, SparseCore 0:
  10.7 71.7 all-gather.2
  85.3 114.9 all-gather.4
  203.3 18.7 all-reduce.2
  224.2 9.5 reduce-scatter.1
where the time goes:
time: 268 us; the launch traced here: 267 us
  waiting for transfers between devices  198 us (74%)
  matrix products  48 us (18%)
  between operations  14.5 us (5%)
  other arithmetic  6.77 us (3%)
    all_gather x1, waiting for transfers between devices, local(): grad_all = lax.all_gather(grad_output, 'dp', axis=0, tiled=True)  116 us
    all_gather x1, waiting for transfers between devices, local(): input_all = lax.all_gather(layer_input, 'dp', axis=0, tiled=True)  73.8 us
    dot_general x3, matrix products, contract_rows(): lax.dot_general(left, right, (((0,), (0,)), ((), ())), preferred_element_...  37 us
    dot_general x1, matrix products, contract_cols(): lax.dot_general(left, right, (((1,), (1,)), ((), ())), preferred_element_...  11 us
    psum x1, waiting for transfers between devices, from_root(): return lax.psum(kept, axis)  7.16 us
  transfers between devices with their start and end apart: 4, of which 3 were waited for; matrix products, arithmetic and copies ran while one was open for 19% of the time, Pallas kernels for 0%

commit v1 on v0

--- a/solution.py
+++ b/solution.py
@@ -1,7 +1,25 @@
+import functools
+
 import jax
 import jax.numpy as jnp
 from jax import lax
+from jax.experimental import pallas as pl
+from jax.experimental.pallas import tpu as pltpu
 from jax.sharding import PartitionSpec as P
+
+LANES = 128
+
+
+def contract_rows(left, right):
+    return lax.dot_general(
+        left, right, (((0,), (0,)), ((), ())), preferred_element_type=jnp.float32
+    )
+
+
+def contract_cols(left, right):
+    return lax.dot_general(
+        left, right, (((1,), (1,)), ((), ())), preferred_element_type=jnp.float32
+    )
 
 
 def from_root(value, axis, source):
@@ -9,16 +27,160 @@
     return lax.psum(kept, axis)
 
 
-def contract_rows(left, right):
-    return lax.dot_general(
-        left, right, (((0,), (0,)), ((), ())), preferred_element_type=jnp.float32
-    )
-
-
-def contract_cols(left, right):
-    return lax.dot_general(
-        left, right, (((1,), (1,)), ((), ())), preferred_element_type=jnp.float32
-    )
+def cuts_of(width):
+    tiles = width // LANES
+    ends = [tiles * i // 4 * LANES for i in range(5)]
+    return [(ends[i], ends[i + 1] - ends[i]) for i in range(4)]
+
+
+def gather_kernel(count, own_ref, all_ref, send_sem, recv_sem, copy_sem):
+    ring_size = count // 4
+    half = ring_size // 2
+    me = lax.axis_index("dp")
+    ring, quad = me // 4, me % 4
+    x_bit, y_bit = quad % 2, quad // 2
+    quad_x = quad + 1 - 2 * x_bit
+    quad_y = quad + 2 - 4 * y_bit
+    quad_d = quad_x + 2 - 4 * y_bit
+    cuts = cuts_of(own_ref.shape[1])
+
+    def at(offset, q):
+        return (ring + offset + ring_size) % ring_size * 4 + q
+
+    up, down, across, along = at(1, quad), at(-1, quad), at(0, quad_x), at(0, quad_y)
+
+    barrier = pltpu.get_barrier_semaphore()
+    for peer in (up, down, across, along):
+        pl.semaphore_signal(
+            barrier, inc=1, device_id={"dp": peer}, device_id_type=pl.DeviceIdType.MESH
+        )
+    pl.semaphore_wait(barrier, 4)
+
+    keep = pltpu.make_async_copy(own_ref, all_ref.at[me], copy_sem)
+    keep.start()
+    sent = []
+    ports = {"up": (0, up), "down": (1, down), "across": (2, across), "along": (3, along)}
+
+    def copy(piece, source, port, mine):
+        lane, target = ports[port]
+        start, size = cuts[piece]
+        columns = pl.ds(start, size)
+        from_ref = own_ref.at[:, columns] if mine else all_ref.at[source, :, columns]
+        return pltpu.make_async_remote_copy(
+            src_ref=from_ref,
+            dst_ref=all_ref.at[source, :, columns],
+            send_sem=send_sem.at[piece, source, lane],
+            recv_sem=recv_sem.at[piece, source],
+            device_id={"dp": target},
+            device_id_type=pl.DeviceIdType.MESH,
+        )
+
+    def send(piece, source, port, mine=False):
+        item = copy(piece, source, port, mine)
+        item.start()
+        sent.append(item)
+
+    def arrive(piece, source):
+        copy(piece, source, "up", False).wait_recv()
+
+    def ring_step(piece, step, q, then=()):
+        turn = piece % 2
+        for sign, port, wins in ((-1, "up", 0), (1, "down", 1)):
+            if step == half and turn != wins:
+                continue
+            source = at(sign * step, q)
+            arrive(piece, source)
+            if step + 1 < half or (step + 1 == half and turn == wins):
+                send(piece, source, port)
+            for other in then:
+                send(piece, source, other)
+
+    def square_step(piece, offset, first, then=()):
+        turn = piece % 2
+        if first:
+            for q, port, wins in ((quad_x, "along", 0), (quad_y, "across", 1)):
+                source = at(offset, q)
+                arrive(piece, source)
+                if turn == wins:
+                    send(piece, source, port)
+                for other in then:
+                    send(piece, source, other)
+        else:
+            source = at(offset, quad_d)
+            arrive(piece, source)
+            for other in then:
+                send(piece, source, other)
+
+    both, flat = ("up", "down"), ("across", "along")
+    for piece in (0, 1):
+        for port in both:
+            send(piece, me, port, True)
+    for piece in (2, 3):
+        for port in flat:
+            send(piece, me, port, True)
+    for piece in (2, 3):
+        for port in both:
+            send(piece, me, port, True)
+    for piece in (0, 1):
+        for port in flat:
+            send(piece, me, port, True)
+    for piece in (0, 1):
+        ring_step(piece, 1, quad, flat)
+    for piece in (2, 3):
+        square_step(piece, 0, True, both)
+    for piece in (2, 3):
+        square_step(piece, 0, False, both)
+    for piece in (0, 1):
+        square_step(piece, 0, True)
+    for step in range(2, half + 1):
+        for piece in (0, 1):
+            ring_step(piece, step, quad, flat)
+    offsets = [sign * step for step in range(1, half) for sign in (-1, 1)] + [half]
+    steps = range(1, half + 1)
+    flat_work = [
+        functools.partial(square_step, piece, offset, True)
+        for offset in offsets
+        for piece in (0, 1)
+    ]
+    ring_work = [
+        functools.partial(ring_step, piece, step, q)
+        for step in steps
+        for q in (quad, quad_x, quad_y, quad_d)
+        for piece in (2, 3)
+    ]
+    done = 0
+    for index, work in enumerate(ring_work):
+        work()
+        goal = len(flat_work) * (index + 1) // len(ring_work)
+        while done < goal:
+            flat_work[done]()
+            done += 1
+    for offset in [0] + offsets:
+        for piece in (0, 1):
+            square_step(piece, offset, False)
+    for item in sent:
+        item.wait_send()
+    keep.wait()
+
+
+def gather(block):
+    count = lax.axis_size("dp")
+    rows, width = block.shape
+    if count % 8 or count < 16:
+        return lax.all_gather(block, "dp", axis=0, tiled=True)
+    everything = pl.pallas_call(
+        functools.partial(gather_kernel, count),
+        out_shape=jax.ShapeDtypeStruct((count, rows, width), block.dtype),
+        in_specs=[pl.BlockSpec(memory_space=pl.ANY)],
+        out_specs=pl.BlockSpec(memory_space=pl.ANY),
+        scratch_shapes=[
+            pltpu.SemaphoreType.DMA((4, count, 4)),
+            pltpu.SemaphoreType.DMA((4, count)),
+            pltpu.SemaphoreType.DMA,
+        ],
+        compiler_params=pltpu.CompilerParams(collective_id=0, has_side_effects=True),
+    )(block)
+    return everything.reshape(count * rows, width)
 
 
 def local(layer_input, up_weight, grad_output, factor_input, factor_grad, decay):
@@ -30,12 +192,17 @@
     blend = (1.0 - keep) / token_total
     feat_rows = up_weight.shape[0]
     unit_rows = factor_grad.shape[0]
-    input_all = lax.all_gather(layer_input, "dp", axis=0, tiled=True)
+    units, feats = grad_output.shape[1], layer_input.shape[1]
+    pad = -(units + feats) % LANES
+    block = jnp.concatenate([grad_output, layer_input], axis=1)
+    block = jnp.pad(block, ((0, 0), (0, pad)))
+    everything = gather(block)
+    grad_all = everything[:, :units]
+    input_all = everything[:, units : units + feats]
     input_slice = lax.dynamic_slice_in_dim(input_all, own % ratio * feat_rows, feat_rows, 1)
     input_part = from_root(input_slice, "tensor", owner)
     gram_input = contract_rows(input_part, input_all)
     new_factor_input = keep * factor_input + blend * gram_input
-    grad_all = lax.all_gather(grad_output, "dp", axis=0, tiled=True)
     grad_slice = lax.dynamic_slice_in_dim(grad_all, own % ratio * unit_rows, unit_rows, 1)
     grad_part = from_root(grad_slice, "tensor", owner)
     grad_weight = contract_rows(input_part, grad_all)

time: 268 us -> 227 us (0.85)
  waiting for transfers between devices: 198 us -> 11.5 us
  Pallas kernels: 0 us -> 136 us
  local copies, waits for them, and re-layouts: 0.01 us -> 9.77 us
    all_gather x2 -> x0, waiting for transfers between devices: 189 us -> none  [the longest x1 116 us: local(): grad_all = lax.all_gather(grad_output, 'dp', axis=0, tiled=True)]
    pallas_call x0 -> x1, Pallas kernels: none -> 136 us  [gather(): pl.pallas_call(functools.partial(gather_kernel, count), out_shape=jax.Sha...]
    slice x0 -> x2, local copies, waits for them, and re-layouts: none -> 9.77 us  [the longest x1 7.63 us: local(): grad_all = everything[:, :units]]
    psum x1, waiting for transfers between devices: 7.16 us -> 11.4 us  [from_root(): return lax.psum(kept, axis)]
  transfers between devices with their start and end apart: 4 -> 2, of which waited for: 3 -> 1; matrix products, arithmetic and copies ran while one was open for 19% -> 21% of each run, Pallas kernels for 0% -> 0%
where the time goes in v1:
time: 227 us
  Pallas kernels  136 us (60%)
  matrix products  47.5 us (21%)
  between operations  14.8 us (7%)
  waiting for transfers between devices  11.5 us (5%)
  local copies, waits for them, and re-layouts  9.77 us (4%)
  other arithmetic  7.77 us (3%)
    pallas_call x1, Pallas kernels, gather(): pl.pallas_call(functools.partial(gather_kernel, count), out_shape=jax.Sha...  136 us
    dot_general x3, matrix products, contract_rows(): lax.dot_general(left, right, (((0,), (0,)), ((), ())), preferred_element_...  37 us
    psum x1, waiting for transfers between devices, from_root(): return lax.psum(kept, axis)  11.4 us
    dot_general x1, matrix products, contract_cols(): lax.dot_general(left, right, (((1,), (1,)), ((), ())), preferred_element_...  10.5 us
    slice x1, local copies, waits for them, and re-layouts, local(): grad_all = everything[:, :units]  7.63 us
  transfers between devices with their start and end apart: 2, of which 1 were waited for; matrix products, arithmetic and copies ran while one was open for 21% of the time, Pallas kernels for 0%

profile of v1, /device:TPU:0, one launch (start us, length us, event | category | flops | bytes accessed | tf_op | source)
XLA Modules:
  0.0 226.9 jit_solution(15802990786314288784)
XLA Ops:
  7.2 0.0 all-reduce.3.cloned.1.call-start
  7.2 2.1 pad_maximum_fusion.own_ref
  9.3 135.6 %shard_map.93 = bf16[16,40,9472]{2,1,0:T(8,128)(2,1)} custom-call(bf16[40,9472]{1,0:T(8,128)(2,1)} %pad_maximum_fusion.own_ref), custom_call_target="tpu_custom_call" | custom-call | tf_op jit(solution)/shard_map/pallas_call | solution.py:171
  144.9 7.6 %slice.9 = bf16[640,6912]{1,0:T(8,128)(2,1)} slice(bf16[640,9472]{1,0:T(8,128)(2,1)} %bitcast.9), slice={[0:640], [0:6912]} | slice | bytes 17694720 | tf_op jit(solution)/shard_map/slice | solution.py:200
  152.5 2.1 slice.8
  154.7 2.9 %dynamic-slice_select_fusion = bf16[640,864]{1,0:T(8,128)(2,1)} fusion(bf16[640,6912]{1,0:T(8,128)(2,1)} %slice.9, s32[]{:T(128)S(6)} %select_n.41, pred[]{:T(512)S(6)} %eq.7), kind=kLoop, calls=%fused_computation.3 | loop fusion | flops 552960 | bytes 2211845 | tf_op jit(solution)/shard_map/jit(_where)/select_n | solution.py:26
  157.6 1.0 dynamic-slice_select_fusion.1
  158.6 0.0 all-reduce.3.cloned.1.call-update
  158.7 0.0 reduce-scatter.2.cloned.1.call-start
  158.7 10.5 %fusion.3 = f32[640,320]{1,0:T(8,128)} fusion(bf16[320,6912]{1,0:T(8,128)(2,1)} %param.7, bf16[640,9472]{1,0:T(8,128)(2,1)} %bitcast.11), kind=kOutput, calls=%fused_computation.8 | convolution fusion | flops 2831155200 | bytes 14090240 | tf_op jit(solution)/shard_map/dot_general | solution.py:20
  169.2 0.0 reduce-scatter.2.cloned.1.call-update
  169.9 11.4 %all-reduce.3.cloned.1.call-done = (bf16[640,320]{1,0:T(8,128)(2,1)}, bf16[640,864]{1,0:T(8,128)(2,1)}) async-done(((bf16[640,320]{1,0:T(8,128)(2,1)}, bf16[640,864]{1,0:T(8,128)(2,1)}), (bf16[640,320]{1,0:T(8,128)(2,1)}, bf16[640,864]{1,0:T(8,128)(2,1)})) %all-reduce.3.cloned.1.call-update) | async-done | bytes 1515536 | tf_op jit(solution)/shard_map/psum | solution.py:27
  181.3 0.0 copy-start
  181.3 21.0 %multiply_add_fusion = f32[864,6912]{1,0:T(8,128)} fusion(f32[864,6912]{1,0:T(8,128)} %param.10, bf16[640,864]{1,0:T(8,128)(2,1)} %get-tuple-element.5, f32[]{:T(128)S(6)} %div.14, f32[]{:T(128)} %bitcast.8, bf16[640,9472]{1,0:T(8,128)(2,1)} %bitcast.12), kind=kOutput, calls=%fused_computation | convolution fusion | flops 7662034944 | bytes 57770500 | tf_op jit(solution)/shard_map/dot_general | solution.py:14
  202.3 0.0 copy-start.1
  202.3 0.0 copy-done
  202.3 5.3 %fusion = f32[320,2560]{1,0:T(8,128)} fusion(bf16[640,320]{1,0:T(8,128)(2,1)} %get-tuple-element.4, f32[320,2560]{1,0:T(8,128)S(1)} %copy-done, f32[]{:T(128)S(6)} %div.14, f32[]{:T(128)} %bitcast.6, bf16[640,9472]{1,0:T(8,128)(2,1)} %bitcast.13), kind=kOutput, calls=%fused_computation.2 | convolution fusion | flops 1051033600 | bytes 10322436 | tf_op jit(solution)/shard_map/dot_general | solution.py:14
  207.6 0.0 copy-done.1
  207.6 10.7 %fusion.5 = f32[320,6912]{1,0:T(8,128)} fusion(bf16[640,320]{1,0:T(8,128)(2,1)S(1)} %copy-done.1, bf16[640,9472]{1,0:T(8,128)(2,1)} %bitcast.14), kind=kOutput, calls=%fused_computation.10 | convolution fusion | flops 2831155200 | bytes 18104320 | tf_op jit(solution)/shard_map/dot_general | solution.py:14
  218.3 0.0 reduce-scatter.2.cloned.1.call-done
  218.3 1.8 convert_element_type.7
Async XLA Ops:
  7.2 174.1 %all-reduce.3.cloned.1.call-start = ((), (), s32[]{:S(2)}) async-start(), calls=%async_computation.2 | async-start | bytes 3276800 | tf_op jit(solution)/shard_map/psum | solution.py:27
  158.7 59.7 %reduce-scatter.2.cloned.1.call-start = ((), (), s32[]{:S(2)}) async-start(), calls=%async_computation.1 | async-start | bytes 1474560 | tf_op jit(solution)/shard_map/reduce_scatter | solution.py:212
  181.3 21.0 %copy-start = (f32[320,2560]{1,0:T(8,128)S(1)}, f32[320,2560]{1,0:T(8,128)}, u32[]{:S(2)}) copy-start(f32[320,2560]{1,0:T(8,128)} %param.9) | copy-start | bytes 9830404
  202.3 5.3 %copy-start.1 = (bf16[640,320]{1,0:T(8,128)(2,1)S(1)}, bf16[640,320]{1,0:T(8,128)(2,1)}, u32[]{:S(2)}) copy-start(bf16[640,320]{1,0:T(8,128)(2,1)} %get-tuple-element.4) | copy-start | bytes 1228804
Sparse Core Ops, SparseCore 0:
  158.8 22.4 all-reduce.2
  183.6 9.5 reduce-scatter.1

commit v2 on v0

v2 whole, which is shorter than its diff:
```python
import functools

import jax
import jax.numpy as jnp
from jax import lax
from jax.experimental import pallas as pl
from jax.experimental.pallas import tpu as pltpu
from jax.sharding import PartitionSpec as P

LANES = 128


def contract_rows(left, right):
    return lax.dot_general(
        left, right, (((0,), (0,)), ((), ())), preferred_element_type=jnp.float32
    )


def contract_cols(left, right):
    return lax.dot_general(
        left, right, (((1,), (1,)), ((), ())), preferred_element_type=jnp.float32
    )


def pieces_of(start, tiles):
    long = tiles * 7 // 18
    short = tiles // 2 - long
    sizes = [long, tiles - long - 2 * short, short, short]
    edges = [start]
    for size in sizes:
        edges.append(edges[-1] + size)
    return [(edges[i] * LANES, sizes[i] * LANES) for i in range(4)]


def jobs_of(widths):
    jobs = []
    for array, width in enumerate(widths):
        tiles = width // LANES
        chunks = max(1, tiles // 18)
        for i in range(chunks):
            start, end = tiles * i // chunks, tiles * (i + 1) // chunks
            jobs.append((array, pieces_of(start, end - start)))
    return jobs


def window_of(own, size, width):
    wide = min(-(-(size + LANES) // LANES) * LANES, width)
    first = jnp.minimum(own * size // LANES * LANES, width - wide)
    return first, wide


def gather_kernel(count, cores, parts, *refs):
    own_refs, all_refs, win_refs = refs[:2], refs[2:4], refs[4:6]
    send_sem, recv_sem, copy_sem, win_send, win_recv = refs[6:]
    length = count // 4
    me = lax.axis_index("dp")
    core = lax.axis_index("tensor")
    line, quad = me // 4, me % 4
    x_bit, y_bit = quad % 2, quad // 2
    quad_x = quad + 1 - 2 * x_bit
    quad_y = quad + 2 - 4 * y_bit
    quad_d = quad_x + 2 - 4 * y_bit
    jobs = jobs_of([ref.shape[1] for ref in own_refs])

    def at(offset, q):
        return (line + offset + length) % length * 4 + q

    targets = [at(1, quad), at(-1, quad), at(0, quad_x), at(0, quad_y)]
    UP, DOWN, ACROSS, ALONG = range(4)
    has = {UP: line < length - 1, DOWN: line > 0}

    barrier = pltpu.get_barrier_semaphore()

    def greet(**where):
        pl.semaphore_signal(
            barrier, inc=1, device_id=where, device_id_type=pl.DeviceIdType.MESH
        )

    for target in targets:
        greet(dp=target)
    for hop in range(1, cores):
        greet(tensor=(core + hop) % cores)
    pl.semaphore_wait(barrier, 4 + cores - 1)

    keeps = [
        pltpu.make_async_copy(own, everything.at[me], copy_sem.at[i])
        for i, (own, everything) in enumerate(zip(own_refs, all_refs))
    ]
    for keep in keeps:
        keep.start()
    sent = []

    def copy(job, piece, source, port, mine=False):
        array, pieces = jobs[job]
        start, size = pieces[piece]
        columns = pl.ds(start, size)
        from_ref = own_refs[array].at[:, columns] if mine else all_refs[array].at[source, :, columns]
        return pltpu.make_async_remote_copy(
            src_ref=from_ref,
            dst_ref=all_refs[array].at[source, :, columns],
            send_sem=send_sem.at[job, piece, source, port],
            recv_sem=recv_sem.at[job, piece, source],
            device_id={"dp": targets[port]},
            device_id_type=pl.DeviceIdType.MESH,
        )

    def under(condition, work):
        if condition is None:
            work()
        else:
            pl.when(condition)(work)

    def both_of(first, second):
        if first is None or second is None:
            return second if first is None else first
        return jnp.logical_and(first, second)

    def send(job, piece, source, ports, exists=None, mine=False):
        for port in ports:
            item = copy(job, piece, source, port, mine)
            condition = both_of(exists, has.get(port))
            under(condition, item.start)
            sent.append((condition, item))

    def arrive(job, piece, source, exists=None):
        under(exists, lambda: copy(job, piece, source, UP).wait_recv())

    def seen(offset):
        if offset == 0:
            return None
        return line >= -offset if offset < 0 else line < length - offset

    def line_step(job, piece, offset, q, then=()):
        source, exists = at(offset, q), seen(offset)
        arrive(job, piece, source, exists)
        send(job, piece, source, (UP if offset < 0 else DOWN,) + tuple(then), exists)

    def square_step(job, piece, offset, q, port, then=()):
        source, exists = at(offset, q), seen(offset)
        arrive(job, piece, source, exists)
        send(job, piece, source, (() if port is None else (port,)) + tuple(then), exists)

    zed, flat = (UP, DOWN), (ACROSS, ALONG)
    offsets = [sign * step for step in range(1, length) for sign in (-1, 1)]

    def start_of(job):
        for pieces, ports in (((0, 1), zed), ((2, 3), flat), ((2, 3), zed), ((0, 1), flat)):
            for piece in pieces:
                send(job, piece, me, ports, mine=True)

    def steps_of(job):
        def near(piece, offset, then=()):
            turn = piece % 2
            square_step(job, piece, offset, quad_x, ALONG if turn == 0 else None, then)
            square_step(job, piece, offset, quad_y, ACROSS if turn == 1 else None, then)

        steps = []

        def add(work, *args):
            steps.append(functools.partial(work, *args))

        for piece in (2, 3):
            add(near, piece, 0, zed)
        for offset in offsets[:2]:
            for piece in (0, 1):
                add(line_step, job, piece, offset, quad, flat)
        for piece in (2, 3):
            add(square_step, job, piece, 0, quad_d, None, zed)
        for piece in (0, 1):
            add(near, piece, 0)
        for offset in offsets[:2]:
            for q in (quad, quad_x):
                for piece in (2, 3):
                    add(line_step, job, piece, offset, q)
            for piece in (0, 1):
                add(near, piece, offset)
        for piece in (0, 1):
            add(square_step, job, piece, 0, quad_d, None)
        for index in range(2, len(offsets) + 2, 2):
            later = offsets[index : index + 2]
            for offset in later:
                for piece in (0, 1):
                    add(line_step, job, piece, offset, quad, flat)
            for offset in offsets[index - 2 : index]:
                for q in (quad_y, quad_d):
                    for piece in (2, 3):
                        add(line_step, job, piece, offset, q)
                for piece in (0, 1):
                    add(square_step, job, piece, offset, quad_d, None)
            for offset in later:
                for q in (quad, quad_x):
                    for piece in (2, 3):
                        add(line_step, job, piece, offset, q)
                for piece in (0, 1):
                    add(near, piece, offset)
        return steps

    ratio = count // cores
    owner = me // ratio
    windows = []
    for array in range(2):
        first, wide = window_of(me % ratio, parts[array], all_refs[array].shape[2])
        first = pl.multiple_of(first, LANES)
        hops = []
        for hop in range(1, cores):
            hops.append(
                pltpu.make_async_remote_copy(
                    src_ref=all_refs[array].at[:, :, pl.ds(first, wide)],
                    dst_ref=win_refs[array],
                    send_sem=win_send.at[array, hop],
                    recv_sem=win_recv.at[array],
                    device_id={"tensor": (core + hop) % cores},
                    device_id_type=pl.DeviceIdType.MESH,
                )
            )
        windows.append(hops)

    def share(array):
        keeps[array].wait()

        @pl.when(core == owner)
        def _():
            for hop in windows[array]:
                hop.start()

    for job in range(len(jobs)):
        start_of(job)
    plan = []
    for job in range(len(jobs)):
        steps = steps_of(job)
        for index, work in enumerate(steps):
            plan.append((index + job * 0.6 * len(steps), job, index == len(steps) - 1, work))
    plan.sort(key=lambda entry: entry[:2])
    left = [sum(1 for array, _ in jobs if array == i) for i in range(2)]
    for _, job, last, work in plan:
        work()
        if last:
            array = jobs[job][0]
            left[array] -= 1
            if left[array] == 0:
                share(array)
    for condition, item in sent:
        under(condition, item.wait_send)
    for hops in windows:

        @pl.when(core == owner)
        def _():
            for hop in hops:
                hop.wait_send()

        @pl.when(core != owner)
        def _():
            hops[0].wait_recv()


def gather(blocks, parts):
    count, cores = lax.axis_size("dp"), lax.axis_size("tensor")
    rows = blocks[0].shape[0]
    widths = [block.shape[1] for block in blocks]
    blocks = [jnp.pad(block, ((0, 0), (0, -block.shape[1] % LANES))) for block in blocks]
    own = lax.axis_index("dp") % (count // cores)
    spans = [window_of(own, part, block.shape[1]) for part, block in zip(parts, blocks)]
    jobs = len(jobs_of([block.shape[1] for block in blocks]))
    shapes = [block.shape[1] for block in blocks] + [wide for _, wide in spans]
    results = pl.pallas_call(
        functools.partial(gather_kernel, count, cores, parts),
        out_shape=[
            jax.ShapeDtypeStruct((count, rows, width), blocks[0].dtype) for width in shapes
        ],
        in_specs=[pl.BlockSpec(memory_space=pl.ANY)] * 2,
        out_specs=[pl.BlockSpec(memory_space=pl.ANY)] * 4,
        scratch_shapes=[
            pltpu.SemaphoreType.DMA((jobs, 4, count, 4)),
            pltpu.SemaphoreType.DMA((jobs, 4, count)),
            pltpu.SemaphoreType.DMA((2,)),
            pltpu.SemaphoreType.DMA((2, cores)),
            pltpu.SemaphoreType.DMA((2,)),
        ],
        compiler_params=pltpu.CompilerParams(collective_id=0, has_side_effects=True),
    )(*blocks)
    flat = [result.reshape(count * rows, result.shape[2]) for result in results]
    here = lax.axis_index("tensor") == lax.axis_index("dp") // (count // cores)
    slices = []
    for everything, window, part, (first, wide) in zip(flat[:2], flat[2:], parts, spans):
        mine = lax.dynamic_slice_in_dim(everything, own * part, part, 1)
        other = lax.dynamic_slice_in_dim(window, own * part - first, part, 1)
        slices.append(jnp.where(here, mine, other))
    whole = [everything[:, :width] for everything, width in zip(flat[:2], widths)]
    return whole, slices


def local(layer_input, up_weight, grad_output, factor_input, factor_grad, decay):
    token_total = layer_input.shape[0] * lax.axis_size("dp")
    keep = decay[0]
    blend = (1.0 - keep) / token_total
    feat_rows = up_weight.shape[0]
    unit_rows = factor_grad.shape[0]
    (input_all, grad_all), (input_part, grad_part) = gather(
        (layer_input, grad_output), (feat_rows, unit_rows)
    )
    gram_input = contract_rows(input_part, input_all)
    new_factor_input = keep * factor_input + blend * gram_input
    grad_weight = contract_rows(input_part, grad_all)
    gram_grad = contract_rows(grad_part, grad_all)
    partial_in = contract_cols(grad_all, up_weight)
    new_factor_grad = keep * factor_grad + blend * gram_grad
    grad_input = lax.psum_scatter(partial_in, "tensor", scatter_dimension=0, tiled=True).astype(
        jnp.bfloat16
    )
    return (grad_weight, grad_input, new_factor_input, new_factor_grad)


def solution(mesh):
    return jax.shard_map(
        local,
        mesh=mesh,
        in_specs=(
            P("dp", "tensor"),
            P("dp", "tensor"),
            P("dp", "tensor"),
            P("dp", "tensor"),
            P("dp", "tensor"),
            P(),
        ),
        out_specs=(P("dp", "tensor"), P("tensor", "dp"), P("dp", "tensor"), P("dp", "tensor")),
        check_vma=False,
    )
```

time: 268 us -> 180 us (0.67)
  waiting for transfers between devices: 198 us -> 0.02 us
  Pallas kernels: 0 us -> 114 us
  other arithmetic: 6.77 us -> 1.75 us
    all_gather x2 -> x0, waiting for transfers between devices: 189 us -> none  [the longest x1 116 us: local(): grad_all = lax.all_gather(grad_output, 'dp', axis=0, tiled=True)]
    pallas_call x0 -> x1, Pallas kernels: none -> 114 us  [gather(): pl.pallas_call(functools.partial(gather_kernel, count, cores, parts), out...]
    psum x1 -> x0, waiting for transfers between devices: 7.16 us -> none  [from_root(): return lax.psum(kept, axis)]
    select_n x2 -> x0, other arithmetic: 5.02 us -> none  [from_root(): jnp.where(lax.axis_index(axis) == source, value, 0).astype(value.dtype)]
  transfers between devices with their start and end apart: 4 -> 1, of which waited for: 3 -> 0; matrix products, arithmetic and copies ran while one was open for 19% -> 22% of each run, Pallas kernels for 0% -> 0%
where the time goes in v2:
time: 180 us
  Pallas kernels  114 us (63%)
  matrix products  49.9 us (28%)
  between operations  14.8 us (8%)
    pallas_call x1, Pallas kernels, gather(): pl.pallas_call(functools.partial(gather_kernel, count, cores, parts), out...  114 us
    dot_general x3, matrix products, contract_rows(): lax.dot_general(left, right, (((0,), (0,)), ((), ())), preferred_element_...  39.5 us
    dot_general x1, matrix products, contract_cols(): lax.dot_general(left, right, (((1,), (1,)), ((), ())), preferred_element_...  10.5 us
  transfers between devices with their start and end apart: 1, of which 0 were waited for; matrix products, arithmetic and copies ran while one was open for 22% of the time, Pallas kernels for 0%

profile of v2, /device:TPU:0, one launch (start us, length us, event | category | flops | bytes accessed | tf_op | source)
XLA Modules:
  0.0 180.3 jit_solution(4316060894604538582)
XLA Ops:
  7.2 0.0 reduce-scatter.2.cloned.1.call-start
  7.2 113.8 %shard_map.93 = (bf16[16,40,2560]{2,1,0:T(8,128)(2,1)}, bf16[16,40,6912]{2,1,0:T(8,128)(2,1)}, bf16[16,40,512]{2,1,0:T(8,128)(2,1)}, bf16[16,40,1024]{2,1,0:T(8,128)(2,1)}) custom-call(bf16[40,2560]{1,0:T(8,128)(2,1)} %refs_0_.1, bf16[40,6912]{1,0:T(8,128)(2,1)} %refs_1_.1), custom_call_target="tpu_custom_call" | custom-call | tf_op jit(solution)/shard_map/pallas_call | solution.py:265
  121.0 10.5 %fusion.9 = f32[640,320]{1,0:T(8,128)} fusion(bf16[640,6912]{1,0:T(8,128)(2,1)} %bitcast.13, bf16[320,6912]{1,0:T(8,128)(2,1)} %param.7), kind=kOutput, calls=%fused_computation.12 | convolution fusion | flops 2831155200 | bytes 14090240 | tf_op jit(solution)/shard_map/dot_general | solution.py:20
  131.4 0.0 reduce-scatter.2.cloned.1.call-update
  132.2 0.0 copy-start
  132.2 23.0 %multiply_add_fusion = f32[864,6912]{1,0:T(8,128)} fusion(f32[864,6912]{1,0:T(8,128)} %param.10, bf16[640,6912]{1,0:T(8,128)(2,1)} %bitcast.14, f32[]{:T(128)S(6)} %div.31, f32[]{:T(128)} %bitcast.12, bf16[640,1024]{1,0:T(8,128)(2,1)} %bitcast.20, s32[]{:T(128)S(6)} %select_n.55, s32[]{:T(128)S(6)} %select_n.53, pred[]{:T(512)S(6)} %eq.5), kind=kOutput, calls=%fused_computation | convolution fusion | flops 7662587904 | bytes 58917388 | tf_op jit(solution)/shard_map/dot_general | solution.py:14
  155.2 0.0 copy-done
  155.2 0.0 copy-start.1
  155.2 5.6 %fusion = f32[320,2560]{1,0:T(8,128)} fusion(bf16[640,2560]{1,0:T(8,128)(2,1)S(1)} %bitcast.16, f32[320,2560]{1,0:T(8,128)} %param.9, f32[]{:T(128)S(6)} %div.31, f32[]{:T(128)} %bitcast.10, bf16[640,512]{1,0:T(8,128)(2,1)} %bitcast.18, s32[]{:T(128)S(6)} %select_n.50, s32[]{:T(128)S(6)} %select_n.48, pred[]{:T(512)S(6)} %eq.5), kind=kOutput, calls=%fused_computation.2 | convolution fusion | flops 1051238400 | bytes 10813965 | tf_op jit(solution)/shard_map/dot_general | solution.py:14
  160.8 0.0 copy-done.1
  160.8 10.9 %fusion.5 = f32[320,6912]{1,0:T(8,128)} fusion(bf16[640,6912]{1,0:T(8,128)(2,1)} %bitcast.15, bf16[640,512]{1,0:T(8,128)(2,1)S(1)} %bitcast.19, s32[]{:T(128)S(6)} %select_n.50, bf16[640,2560]{1,0:T(8,128)(2,1)S(1)} %bitcast.17, s32[]{:T(128)S(6)} %select_n.48, pred[]{:T(512)S(6)} %eq.5), kind=kOutput, calls=%fused_computation.8 | convolution fusion | flops 2831360000 | bytes 18677768 | tf_op jit(solution)/shard_map/dot_general | solution.py:14
  171.7 0.0 reduce-scatter.2.cloned.1.call-done
  171.7 1.8 convert_element_type.3
Async XLA Ops:
  7.2 164.5 %reduce-scatter.2.cloned.1.call-start = ((), (), s32[]{:S(2)}) async-start(), calls=%async_computation.1 | async-start | bytes 1474560 | tf_op jit(solution)/shard_map/reduce_scatter | solution.py:307
  132.2 23.0 %copy-start = (bf16[16,40,2560]{2,1,0:T(8,128)(2,1)S(1)}, bf16[16,40,2560]{2,1,0:T(8,128)(2,1)}, u32[]{:S(2)}) copy-start(bf16[16,40,2560]{2,1,0:T(8,128)(2,1)} %get-tuple-element.8) | copy-start | bytes 9830404
  155.2 5.6 %copy-start.1 = (bf16[16,40,512]{2,1,0:T(8,128)(2,1)S(1)}, bf16[16,40,512]{2,1,0:T(8,128)(2,1)}, u32[]{:S(2)}) copy-start(bf16[16,40,512]{2,1,0:T(8,128)(2,1)} %get-tuple-element.9) | copy-start | bytes 1966084
Sparse Core Ops, SparseCore 0:
  131.6 5.2 reduce-scatter.1

commit v3 on v2

--- a/solution.py
+++ b/solution.py
@@ -157,7 +157,8 @@
         steps = []
 
         def add(work, *args):
-            steps.append(functools.partial(work, *args))
+            offset = args[1] if work is near else args[2]
+            steps.append((offset, functools.partial(work, *args)))
 
         for piece in (2, 3):
             add(near, piece, 0, zed)
@@ -198,59 +199,50 @@
     ratio = count // cores
     owner = me // ratio
     windows = []
-    for array in range(2):
+
+    def share(array, offset):
+        if offset == 0:
+            keeps[array].wait()
         first, wide = window_of(me % ratio, parts[array], all_refs[array].shape[2])
-        first = pl.multiple_of(first, LANES)
-        hops = []
+        columns = pl.ds(pl.multiple_of(first, LANES), wide)
+        place = (line + offset + length) % length
+        rows = pl.ds(place * 4, 4)
         for hop in range(1, cores):
-            hops.append(
-                pltpu.make_async_remote_copy(
-                    src_ref=all_refs[array].at[:, :, pl.ds(first, wide)],
-                    dst_ref=win_refs[array],
-                    send_sem=win_send.at[array, hop],
-                    recv_sem=win_recv.at[array],
-                    device_id={"tensor": (core + hop) % cores},
-                    device_id_type=pl.DeviceIdType.MESH,
-                )
+            item = pltpu.make_async_remote_copy(
+                src_ref=all_refs[array].at[rows, :, columns],
+                dst_ref=win_refs[array].at[rows],
+                send_sem=win_send.at[array, hop, place],
+                recv_sem=win_recv.at[array, place],
+                device_id={"tensor": (core + hop) % cores},
+                device_id_type=pl.DeviceIdType.MESH,
             )
-        windows.append(hops)
-
-    def share(array):
-        keeps[array].wait()
-
-        @pl.when(core == owner)
-        def _():
-            for hop in windows[array]:
-                hop.start()
+            under(both_of(seen(offset), core == owner), item.start)
+            windows.append((offset, hop, item))
 
     for job in range(len(jobs)):
         start_of(job)
     plan = []
     for job in range(len(jobs)):
         steps = steps_of(job)
-        for index, work in enumerate(steps):
-            plan.append((index + job * 0.6 * len(steps), job, index == len(steps) - 1, work))
+        for index, (offset, work) in enumerate(steps):
+            plan.append((index + job * 0.6 * len(steps), job, offset, work))
     plan.sort(key=lambda entry: entry[:2])
-    left = [sum(1 for array, _ in jobs if array == i) for i in range(2)]
-    for _, job, last, work in plan:
+    left = {}
+    for _, job, offset, _ in plan:
+        key = jobs[job][0], offset
+        left[key] = left.get(key, 0) + 1
+    for _, job, offset, work in plan:
         work()
-        if last:
-            array = jobs[job][0]
-            left[array] -= 1
-            if left[array] == 0:
-                share(array)
+        key = jobs[job][0], offset
+        left[key] -= 1
+        if left[key] == 0:
+            share(*key)
     for condition, item in sent:
         under(condition, item.wait_send)
-    for hops in windows:
-
-        @pl.when(core == owner)
-        def _():
-            for hop in hops:
-                hop.wait_send()
-
-        @pl.when(core != owner)
-        def _():
-            hops[0].wait_recv()
+    for offset, hop, item in windows:
+        under(both_of(seen(offset), core == owner), item.wait_send)
+        if hop == 1:
+            under(both_of(seen(offset), core != owner), item.wait_recv)
 
 
 def gather(blocks, parts):
@@ -273,8 +265,8 @@
             pltpu.SemaphoreType.DMA((jobs, 4, count, 4)),
             pltpu.SemaphoreType.DMA((jobs, 4, count)),
             pltpu.SemaphoreType.DMA((2,)),
-            pltpu.SemaphoreType.DMA((2, cores)),
-            pltpu.SemaphoreType.DMA((2,)),
+            pltpu.SemaphoreType.DMA((2, cores, count // 4)),
+            pltpu.SemaphoreType.DMA((2, count // 4)),
         ],
         compiler_params=pltpu.CompilerParams(collective_id=0, has_side_effects=True),
     )(*blocks)
@@ -287,6 +279,17 @@
         slices.append(jnp.where(here, mine, other))
     whole = [everything[:, :width] for everything, width in zip(flat[:2], widths)]
     return whole, slices
+
+
+def scatter_sum(value, axis):
+    size, me = lax.axis_size(axis), lax.axis_index(axis)
+    rows = value.shape[0] // size
+    total = lax.dynamic_slice_in_dim(value, me * rows, rows, 0)
+    for hop in range(1, size):
+        share = lax.dynamic_slice_in_dim(value, (me + hop) % size * rows, rows, 0)
+        ring = [(i, (i + hop) % size) for i in range(size)]
+        total = total + lax.ppermute(share, axis, ring)
+    return total
 
 
 def local(layer_input, up_weight, grad_output, factor_input, factor_grad, decay):
@@ -304,9 +307,7 @@
     gram_grad = contract_rows(grad_part, grad_all)
     partial_in = contract_cols(grad_all, up_weight)
     new_factor_grad = keep * factor_grad + blend * gram_grad
-    grad_input = lax.psum_scatter(partial_in, "tensor", scatter_dimension=0, tiled=True).astype(
-        jnp.bfloat16
-    )
+    grad_input = scatter_sum(partial_in, "tensor").astype(jnp.bfloat16)
     return (grad_weight, grad_input, new_factor_input, new_factor_grad)
 
 

time: 180 us -> 168 us (0.933)
  between operations: 14.8 us -> 1.36 us
  local copies, waits for them, and re-layouts: 0.01 us -> 2.76 us
  transfers between devices with their start and end apart: 1 -> 1, of which waited for: 0 -> 0; matrix products, arithmetic and copies ran while one was open for 22% -> 23% of each run, Pallas kernels for 0% -> 0%
where the time goes in v3:
time: 168 us; the launch traced here: 167 us
  Pallas kernels  113 us (67%)
  matrix products  49.2 us (29%)
  local copies, waits for them, and re-layouts  2.76 us (2%)
    pallas_call x1, Pallas kernels, gather(): pl.pallas_call(functools.partial(gather_kernel, count, cores, parts), out...  113 us
    dot_general x3, matrix products, contract_rows(): lax.dot_general(left, right, (((0,), (0,)), ((), ())), preferred_element_...  38.9 us
    dot_general x1, matrix products, contract_cols(): lax.dot_general(left, right, (((1,), (1,)), ((), ())), preferred_element_...  10.4 us
  transfers between devices with their start and end apart: 1, of which 0 were waited for; matrix products, arithmetic and copies ran while one was open for 23% of the time, Pallas kernels for 0%

profile of v3, /device:TPU:0, one launch (start us, length us, event | category | flops | bytes accessed | tf_op | source)
XLA Modules:
  0.0 167.4 jit_solution(17243731148933528137)
XLA Ops:
  0.6 112.5 %shard_map.93 = (bf16[16,40,2560]{2,1,0:T(8,128)(2,1)}, bf16[16,40,6912]{2,1,0:T(8,128)(2,1)}, bf16[16,40,512]{2,1,0:T(8,128)(2,1)}, bf16[16,40,1024]{2,1,0:T(8,128)(2,1)}) custom-call(bf16[40,2560]{1,0:T(8,128)(2,1)} %refs_0_.1, bf16[40,6912]{1,0:T(8,128)(2,1)} %refs_1_.1), custom_call_target="tpu_custom_call" | custom-call | tf_op jit(solution)/shard_map/pallas_call | solution.py:257
  113.2 0.0 copy-start
  113.2 10.4 %fusion.9 = f32[640,320]{0,1:T(8,128)S(1)} fusion(bf16[640,6912]{1,0:T(8,128)(2,1)} %bitcast.13, bf16[320,6912]{1,0:T(8,128)(2,1)} %param.7), kind=kOutput, calls=%fused_computation.14 | convolution fusion | flops 2831155200 | bytes 14090240 | tf_op jit(solution)/shard_map/dot_general | solution.py:20
  123.5 0.0 copy-start.1
  123.5 0.9 copy-done.1
  124.4 1.0 constant_dynamic-slice_fusion
  125.4 0.4 collective-permute-start
  126.5 0.0 copy-done
  126.5 11.1 %fusion.5 = f32[320,6912]{1,0:T(8,128)} fusion(bf16[640,6912]{1,0:T(8,128)(2,1)} %bitcast.14, bf16[640,512]{1,0:T(8,128)(2,1)} %bitcast.18, s32[]{:T(128)S(6)} %select_n.60, bf16[640,2560]{1,0:T(8,128)(2,1)S(1)} %bitcast.16, s32[]{:T(128)S(6)} %select_n.58, pred[]{:T(512)S(6)} %eq.6), kind=kOutput, calls=%fused_computation.9 | convolution fusion | flops 2831360000 | bytes 18677768 | tf_op jit(solution)/shard_map/dot_general | solution.py:14
  137.6 22.1 %multiply_add_fusion = f32[864,6912]{1,0:T(8,128)} fusion(f32[864,6912]{1,0:T(8,128)} %param.10, bf16[640,6912]{1,0:T(8,128)(2,1)} %bitcast.15, f32[]{:T(128)S(6)} %div.31, f32[]{:T(128)} %bitcast.12, bf16[640,1024]{1,0:T(8,128)(2,1)} %bitcast.20, s32[]{:T(128)S(6)} %select_n.68, s32[]{:T(128)S(6)} %select_n.66, pred[]{:T(512)S(6)} %eq.6), kind=kOutput, calls=%fused_computation | convolution fusion | flops 7662587904 | bytes 58917388 | tf_op jit(solution)/shard_map/dot_general | solution.py:14
  159.8 0.0 copy-start.2
  159.8 5.6 %fusion = f32[320,2560]{1,0:T(8,128)} fusion(bf16[640,2560]{1,0:T(8,128)(2,1)S(1)} %bitcast.17, f32[320,2560]{1,0:T(8,128)} %param.9, f32[]{:T(128)S(6)} %div.31, f32[]{:T(128)} %bitcast.10, bf16[640,512]{1,0:T(8,128)(2,1)} %bitcast.19, s32[]{:T(128)S(6)} %select_n.60, s32[]{:T(128)S(6)} %select_n.58, pred[]{:T(512)S(6)} %eq.6), kind=kOutput, calls=%fused_computation.2 | convolution fusion | flops 1051238400 | bytes 10813965 | tf_op jit(solution)/shard_map/dot_general | solution.py:14
  165.4 0.0 collective-permute-done
  165.4 0.0 copy-done.2
  165.4 1.2 add_convert_fusion
  166.6 0.9 copy.10
Async XLA Ops:
  113.2 13.3 %copy-start = (bf16[16,40,2560]{2,1,0:T(8,128)(2,1)S(1)}, bf16[16,40,2560]{2,1,0:T(8,128)(2,1)}, u32[]{:S(2)}) copy-start(bf16[16,40,2560]{2,1,0:T(8,128)(2,1)} %get-tuple-element.8) | copy-start | bytes 9830404
  123.5 0.9 copy-start.1
  125.4 39.9 %collective-permute-start = (f32[320,320]{0,1:T(8,128)}, f32[320,320]{0,1:T(8,128)}, u32[]{:S(2)}, u32[]{:S(2)}) collective-permute-start(f32[320,320]{0,1:T(8,128)} %constant_dynamic-slice_fusion), channel_id=1, source_target_pairs={{0,1},{1,0},{2,3},{3,2},{4,5},{5,4},{6,7},{7,6},{8,9},{9,8},{10,11... | collective-permute-start | bytes 1228808 | tf_op jit(solution)/shard_map/ppermute | solution.py:291
  159.8 5.6 %copy-start.2 = (f32[640,320]{0,1:T(8,128)S(1)}, f32[640,320]{0,1:T(8,128)}, u32[]{:S(2)}) copy-start(f32[640,320]{0,1:T(8,128)} %copy-done.1) | copy-start | bytes 2457604

commit v4 on v3

--- a/solution.py
+++ b/solution.py
@@ -36,7 +36,7 @@
     jobs = []
     for array, width in enumerate(widths):
         tiles = width // LANES
-        chunks = max(1, tiles // 18)
+        chunks = max(1, tiles // 108)
         for i in range(chunks):
             start, end = tiles * i // chunks, tiles * (i + 1) // chunks
             jobs.append((array, pieces_of(start, end - start)))

time: 168 us -> 156 us (0.929)
  Pallas kernels: 113 us -> 101 us
    pallas_call x1, Pallas kernels: 113 us -> 101 us  [gather(): pl.pallas_call(functools.partial(gather_kernel, count, cores, parts), out...]
  transfers between devices with their start and end apart: 1 -> 1, of which waited for: 0 -> 0; matrix products, arithmetic and copies ran while one was open for 23% -> 25% of each run, Pallas kernels for 0% -> 0%
where the time goes in v4:
time: 156 us
  Pallas kernels  101 us (65%)
  matrix products  49.2 us (32%)
  local copies, waits for them, and re-layouts  2.76 us (2%)
    pallas_call x1, Pallas kernels, gather(): pl.pallas_call(functools.partial(gather_kernel, count, cores, parts), out...  101 us
    dot_general x3, matrix products, contract_rows(): lax.dot_general(left, right, (((0,), (0,)), ((), ())), preferred_element_...  38.9 us
    dot_general x1, matrix products, contract_cols(): lax.dot_general(left, right, (((1,), (1,)), ((), ())), preferred_element_...  10.4 us
  transfers between devices with their start and end apart: 1, of which 0 were waited for; matrix products, arithmetic and copies ran while one was open for 25% of the time, Pallas kernels for 0%

profile of v4, /device:TPU:0, one launch (start us, length us, event | category | flops | bytes accessed | tf_op | source)
XLA Modules:
  0.0 155.6 jit_solution(8433371037545126276)
XLA Ops:
  0.6 100.6 %shard_map.93 = (bf16[16,40,2560]{2,1,0:T(8,128)(2,1)}, bf16[16,40,6912]{2,1,0:T(8,128)(2,1)}, bf16[16,40,512]{2,1,0:T(8,128)(2,1)}, bf16[16,40,1024]{2,1,0:T(8,128)(2,1)}) custom-call(bf16[40,2560]{1,0:T(8,128)(2,1)} %refs_0_.1, bf16[40,6912]{1,0:T(8,128)(2,1)} %refs_1_.1), custom_call_target="tpu_custom_call" | custom-call | tf_op jit(solution)/shard_map/pallas_call | solution.py:257
  101.3 0.0 copy-start
  101.3 10.4 %fusion.9 = f32[640,320]{0,1:T(8,128)S(1)} fusion(bf16[640,6912]{1,0:T(8,128)(2,1)} %bitcast.13, bf16[320,6912]{1,0:T(8,128)(2,1)} %param.7), kind=kOutput, calls=%fused_computation.14 | convolution fusion | flops 2831155200 | bytes 14090240 | tf_op jit(solution)/shard_map/dot_general | solution.py:20
  111.7 0.0 copy-start.1
  111.7 0.9 copy-done.1
  112.6 1.0 constant_dynamic-slice_fusion
  113.6 0.4 collective-permute-start
  114.6 0.0 copy-done
  114.6 11.1 %fusion.5 = f32[320,6912]{1,0:T(8,128)} fusion(bf16[640,6912]{1,0:T(8,128)(2,1)} %bitcast.14, bf16[640,512]{1,0:T(8,128)(2,1)} %bitcast.18, s32[]{:T(128)S(6)} %select_n.60, bf16[640,2560]{1,0:T(8,128)(2,1)S(1)} %bitcast.16, s32[]{:T(128)S(6)} %select_n.58, pred[]{:T(512)S(6)} %eq.6), kind=kOutput, calls=%fused_computation.9 | convolution fusion | flops 2831360000 | bytes 18677768 | tf_op jit(solution)/shard_map/dot_general | solution.py:14
  125.7 22.1 %multiply_add_fusion = f32[864,6912]{1,0:T(8,128)} fusion(f32[864,6912]{1,0:T(8,128)} %param.10, bf16[640,6912]{1,0:T(8,128)(2,1)} %bitcast.15, f32[]{:T(128)S(6)} %div.31, f32[]{:T(128)} %bitcast.12, bf16[640,1024]{1,0:T(8,128)(2,1)} %bitcast.20, s32[]{:T(128)S(6)} %select_n.68, s32[]{:T(128)S(6)} %select_n.66, pred[]{:T(512)S(6)} %eq.6), kind=kOutput, calls=%fused_computation | convolution fusion | flops 7662587904 | bytes 58917388 | tf_op jit(solution)/shard_map/dot_general | solution.py:14
  147.9 0.0 copy-start.2
  147.9 5.6 %fusion = f32[320,2560]{1,0:T(8,128)} fusion(bf16[640,2560]{1,0:T(8,128)(2,1)S(1)} %bitcast.17, f32[320,2560]{1,0:T(8,128)} %param.9, f32[]{:T(128)S(6)} %div.31, f32[]{:T(128)} %bitcast.10, bf16[640,512]{1,0:T(8,128)(2,1)} %bitcast.19, s32[]{:T(128)S(6)} %select_n.60, s32[]{:T(128)S(6)} %select_n.58, pred[]{:T(512)S(6)} %eq.6), kind=kOutput, calls=%fused_computation.2 | convolution fusion | flops 1051238400 | bytes 10813965 | tf_op jit(solution)/shard_map/dot_general | solution.py:14
  153.5 0.0 collective-permute-done
  153.5 0.0 copy-done.2
  153.5 1.2 add_convert_fusion
  154.7 0.9 copy.10
Async XLA Ops:
  101.3 13.3 %copy-start = (bf16[16,40,2560]{2,1,0:T(8,128)(2,1)S(1)}, bf16[16,40,2560]{2,1,0:T(8,128)(2,1)}, u32[]{:S(2)}) copy-start(bf16[16,40,2560]{2,1,0:T(8,128)(2,1)} %get-tuple-element.8) | copy-start | bytes 9830404
  111.7 0.9 copy-start.1
  113.6 39.9 %collective-permute-start = (f32[320,320]{0,1:T(8,128)}, f32[320,320]{0,1:T(8,128)}, u32[]{:S(2)}, u32[]{:S(2)}) collective-permute-start(f32[320,320]{0,1:T(8,128)} %constant_dynamic-slice_fusion), channel_id=1, source_target_pairs={{0,1},{1,0},{2,3},{3,2},{4,5},{5,4},{6,7},{7,6},{8,9},{9,8},{10,11... | collective-permute-start | bytes 1228808 | tf_op jit(solution)/shard_map/ppermute | solution.py:291
  147.9 5.6 %copy-start.2 = (f32[640,320]{0,1:T(8,128)S(1)}, f32[640,320]{0,1:T(8,128)}, u32[]{:S(2)}) copy-start(f32[640,320]{0,1:T(8,128)} %copy-done.1) | copy-start | bytes 2457604
